TPU v7x, 128 devices: a whole 4x4x4 slice. The times are simulated.
128 devices in a mesh: alpha: 8 (over x, core), beta: 16 (over z, y).
Axes of the slice: x: 4, y: 4, z: 4, core: 2. Of those that a mesh axis runs over, the one named last changes fastest.
Arguments:
- csf_coef: float32 [42, 98304], P(None, ('alpha', 'beta')), may hold values from -18 to 18
- conf_class: int32 [98304], P(('alpha', 'beta')), may hold values from 0 to 5
- conf_tile: int32 [98304, 1], P(('alpha', 'beta')), may hold values from 0 to 127, as said below
- transforms: float32 [6, 42, 256], replicated, may hold values from -1 to 1
- alpha_targets: int32 [16, 12288], P(None, 'alpha'), may hold values from 0 to 12287, as said below
- alpha_values: bfloat16 [16, 12288], P(None, 'alpha'), may hold values from -1.796875 to 1.796875
- alpha_counts: int32 [12288], P('alpha'), may hold values from 1 to 16, as said below
- beta_targets: int32 [16, 6144], P(None, 'beta'), may hold values from 0 to 6143, as said below
- beta_values: bfloat16 [16, 6144], P(None, 'beta'), may hold values from -1.796875 to 1.796875
- beta_counts: int32 [6144], P('beta'), may hold values from 1 to 16, as said below
- det_diag: float32 [12288, 6144], P('alpha', 'beta'), may hold values from 0.5 to 2
Outputs:
- residual: float32 [42, 98304], P(None, ('alpha', 'beta'))
- residual_rms: float32 [], replicated
Inputs may be any that keep to these rules, and one draw needn't show every extreme that they name: `conf_tile`: among the 768 configurations of one device no tile is named more than 18 times; in every draw some tile is named exactly 18 times by the configurations of every device. `alpha_targets`: in each column the 16 entries are distinct and differ from the column's own string. `beta_targets`: in each column the 16 entries are distinct and differ from the column's own string. `alpha_counts`: some string has exactly 16. `beta_counts`: some string has exactly 16.
All inputs are finite; a program needn't handle non-finite values.
Results may differ from a plain program's by a relative error of at most 0.00075.
The roundings to bfloat16 on the way count: a program that leaves them out, or rounds other values in their place, can miss the bound.
Values may be sent and summed in bfloat16 or wider, within the bound.
No kernel may reach another device: no remote copies, remote signals or barrier semaphores. Data moves between devices by JAX's collectives and lax.ppermute only.
A program may use at most 128 MiB of HBM per device.

v0:
```python
import math
import jax
import jax.numpy as jnp
from jax import lax
from jax.sharding import PartitionSpec as P


def class_forward(coefs, classes, transforms):
    summed = jnp.zeros((coefs.shape[1], transforms.shape[2]), jnp.float32)
    for class_id in range(transforms.shape[0]):
        masked = jnp.where(classes[None, :] == class_id, coefs, jnp.zeros_like(coefs))
        summed = summed + lax.dot_general(
            masked,
            transforms[class_id],
            (((0,), (0,)), ((), ())),
            precision=lax.Precision.HIGHEST,
            preferred_element_type=jnp.float32,
        )
    return summed


def class_backward(values, classes, transforms):
    summed = jnp.zeros((transforms.shape[1], values.shape[0]), jnp.float32)
    for class_id in range(transforms.shape[0]):
        product = lax.dot_general(
            transforms[class_id],
            values,
            (((1,), (1,)), ((), ())),
            precision=lax.Precision.HIGHEST,
            preferred_element_type=jnp.float32,
        )
        summed = summed + jnp.where(classes[None, :] == class_id, product, jnp.zeros_like(product))
    return summed


def bucket_slots(chosen_tiles, buckets):
    onehot = (chosen_tiles[:, None] == jnp.arange(buckets, dtype=jnp.int32)[None, :]).astype(
        jnp.int32
    )
    running = jnp.cumsum(onehot, axis=0) - onehot
    return jnp.sum(onehot * running, axis=1)


def live_weights(values, counts):
    active = jnp.arange(values.shape[0], dtype=jnp.int32)[:, None] < counts[None, :]
    return jnp.where(active, values.astype(jnp.float32), jnp.zeros(values.shape, jnp.float32))


def coupling_block(targets, weights, first_row, block_rows, columns):
    block_targets = lax.dynamic_slice_in_dim(targets, first_row, block_rows, 1)
    block_weights = lax.dynamic_slice_in_dim(weights, first_row, block_rows, 1)
    coupling = jnp.zeros((block_rows, columns.shape[0]), jnp.float32)
    for excitation in range(targets.shape[0]):
        coupling = coupling + jnp.where(
            block_targets[excitation][:, None] == columns[None, :],
            block_weights[excitation][:, None],
            jnp.float32(0.0),
        )
    return coupling.astype(jnp.bfloat16)


def alpha_fold(targets, weights, block_rows, summed, gathered):
    columns = jnp.arange(gathered.shape[0], dtype=jnp.int32)

    def alpha_one_block(block_id):
        coupling = coupling_block(targets, weights, block_id * block_rows, block_rows, columns)
        return jnp.dot(coupling, gathered, preferred_element_type=jnp.float32)

    blocks = lax.map(alpha_one_block, jnp.arange(summed.shape[0] // block_rows, dtype=jnp.int32))
    return blocks.reshape(summed.shape)


def beta_fold(targets, weights, block_rows, summed, gathered):
    columns = jnp.arange(gathered.shape[1], dtype=jnp.int32)

    def beta_one_block(block_id):
        coupling = coupling_block(targets, weights, block_id * block_rows, block_rows, columns)
        return lax.dot_general(
            gathered, coupling, (((1,), (1,)), ((), ())), preferred_element_type=jnp.float32
        )

    blocks = lax.map(beta_one_block, jnp.arange(summed.shape[1] // block_rows, dtype=jnp.int32))
    return jnp.moveaxis(blocks, 0, 1).reshape(summed.shape)


def body(
    csf_coef,
    conf_class,
    conf_tile,
    transforms,
    alpha_targets,
    alpha_values,
    alpha_counts,
    beta_targets,
    beta_values,
    beta_counts,
    det_diag,
):
    nalpha = lax.axis_size("alpha")
    beta_devices = lax.axis_size("beta")
    devices = nalpha * beta_devices
    local_confs = csf_coef.shape[1]
    capacity = 3 * local_confs // devices
    rows_alpha, cols_beta = det_diag.shape
    det_width = transforms.shape[2]
    target_tile = conf_tile[:, 0]
    slot_index = bucket_slots(target_tile, devices)
    det_values = class_forward(csf_coef, conf_class, transforms).astype(jnp.bfloat16)
    outgoing = (
        jnp.zeros((devices, capacity, det_width), jnp.bfloat16)
        .at[target_tile, slot_index]
        .set(det_values)
    )
    arrived = lax.all_to_all(outgoing, ("alpha", "beta"), split_axis=0, concat_axis=0, tiled=True)
    amplitude = arrived.reshape(rows_alpha, cols_beta)
    alpha_weights = live_weights(alpha_values, alpha_counts)
    alpha_term = alpha_fold(
        alpha_targets,
        alpha_weights,
        math.gcd(rows_alpha, 256),
        jnp.zeros((rows_alpha, cols_beta), jnp.float32),
        lax.all_gather(amplitude, "alpha", axis=0, tiled=True),
    )
    beta_weights = live_weights(beta_values, beta_counts)
    beta_term = beta_fold(
        beta_targets,
        beta_weights,
        math.gcd(cols_beta, 256),
        jnp.zeros((rows_alpha, cols_beta), jnp.float32),
        lax.all_gather(amplitude, "beta", axis=1, tiled=True),
    )
    sigma_grid = (alpha_term + beta_term + det_diag * amplitude.astype(jnp.float32)).astype(
        jnp.bfloat16
    )
    returned = lax.all_to_all(
        sigma_grid.reshape(devices, capacity, det_width),
        ("alpha", "beta"),
        split_axis=0,
        concat_axis=0,
        tiled=True,
    )
    sigma_dets = returned[target_tile, slot_index].astype(jnp.float32)
    sigma_csf = class_backward(sigma_dets, conf_class, transforms)
    own_square = jnp.sum(csf_coef * csf_coef)
    own_cross = jnp.sum(csf_coef * sigma_csf)
    total_entries = csf_coef.shape[0] * local_confs * devices
    square_sum, cross_sum = lax.psum((own_square, own_cross), ("alpha", "beta"))
    rayleigh = cross_sum / square_sum
    residual = sigma_csf - rayleigh * csf_coef
    residual_square = lax.psum(jnp.sum(residual * residual), ("alpha", "beta"))
    residual_rms = jnp.sqrt(residual_square / total_entries)
    return (residual, residual_rms)


def solution(mesh):
    placed = (
        P(None, ("alpha", "beta")),
        P(("alpha", "beta")),
        P(("alpha", "beta"), None),
        P(),
        P(None, "alpha"),
        P(None, "alpha"),
        P("alpha"),
        P(None, "beta"),
        P(None, "beta"),
        P("beta"),
        P("alpha", "beta"),
    )
    return jax.shard_map(
        body,
        mesh=mesh,
        in_specs=placed,
        out_specs=(P(None, ("alpha", "beta")), P()),
        check_vma=False,
    )
```

profile of v0, /device:TPU:1, one launch (start us, length us, event | category | flops | bytes accessed | tf_op | source)
XLA Modules:
  0.0 629.4 jit_solution(12536454217057345708)
XLA Ops:
  9.5 1.3 fusion.143
  10.8 1.6 fusion.97
  16.9 37.6 %scatter_fusion = bf16[128,18,256]{2,0,1:T(8,128)(2,1)S(1)} fusion(bf16[128,18,256]{2,0,1:T(8,128)(2,1)S(1)} %broadcast_in_dim.410, s32[768]{0:T(1024)S(1)} %get-tuple-element.263, bf16[768,256]{1,0:T(8,128)(2,1)S(1)} %fusion.80), kind=kCustom, calls=%fused_computation.1 | custom fusion | bytes 1185792 | tf_op jit(solution)/shard_map/scatter | solution.py:112
  55.2 35.2 %all_to_all.10 = bf16[128,18,256]{2,1,0:T(8,128)(2,1)S(1)} all-to-all(bf16[128,18,256]{2,1,0:T(8,128)(2,1)S(1)} %copy.27), channel_id=1, replica_groups=mesh['alpha'=8,'beta'=16] {'alpha','beta'}, dimensions={0} | all-to-all | bytes 2359296 | tf_op jit(solution)/shard_map/all_to_all | solution.py:114
  90.4 1.7 reshape.130
  93.5 49.5 %all-gather.3.cloned.1.call-done = bf16[12288,384]{1,0:T(8,128)(2,1)} async-done(((bf16[1536,384]{1,0:T(8,128)(2,1)}), bf16[12288,384]{1,0:T(8,128)(2,1)}) %all-gather.3.cloned.1.call-update) | async-done | bytes 9437200 | tf_op jit(solution)/shard_map/all_gather | solution.py:122
  143.1 233.3 %while.24 = (s32[]{:T(128)}, f32[6,256,384]{2,1,0:T(8,128)}, s32[6]{0:T(128)S(1)}, s32[16,1536]{1,0:T(8,128)}, f32[16,1536]{1,0:T(8,128)S(1)}, /*index=5*/bf16[1...) while((s32[]{:T(128)}, f32[6,256,384]{2,1,0:T(8,128)}, ...), condition=%wide.region_5.6_spmd.clone.clone, body=%wide.region_4.5_spmd.clone.clone.sunk | while | flops 2566914048 | bytes 9929803 | solution.py:69
  163.5 1.4 constant_dynamic-slice_fusion.7
  164.9 31.6 %fusion.159 = f32[6,256,384]{2,1,0:T(8,128)} fusion(f32[6,256,384]{2,1,0:T(8,128)} %get-tuple-element.666, s32[]{:T(128)} %get-tuple-element.665, bf16[12288,384]{1,0:T(8,128)(2,1)} %get-tuple-element.695, f32[256]{0:T(256)S(1)} %bitcast.268, s32[256]{0:T(256)S(1)} %bitcast.284, f32[256]{0:T(256)S(1)} %bitcast.254, s32[256]{0:T(256)S(1)} %bitcast.270, ...), kind=kOutput, calls=%fused_computation.56.clone.1 | convolution fusion | flops 2566914048 | bytes 9863680 | tf_op jit(solution)/shard_map/while/body/eval_jaxpr/dot_general | solution.py:67
  198.0 1.4 constant_dynamic-slice_fusion.7
  199.4 31.8 %fusion.159 = f32[6,256,384]{2,1,0:T(8,128)} fusion(f32[6,256,384]{2,1,0:T(8,128)} %get-tuple-element.666, s32[]{:T(128)} %get-tuple-element.665, bf16[12288,384]{1,0:T(8,128)(2,1)} %get-tuple-element.695, f32[256]{0:T(256)S(1)} %bitcast.268, s32[256]{0:T(256)S(1)} %bitcast.284, f32[256]{0:T(256)S(1)} %bitcast.254, s32[256]{0:T(256)S(1)} %bitcast.270, ...), kind=kOutput, calls=%fused_computation.56.clone.1 | convolution fusion | flops 2566914048 | bytes 9863680 | tf_op jit(solution)/shard_map/while/body/eval_jaxpr/dot_general | solution.py:67
  232.6 1.4 constant_dynamic-slice_fusion.7
  234.0 31.4 %fusion.159 = f32[6,256,384]{2,1,0:T(8,128)} fusion(f32[6,256,384]{2,1,0:T(8,128)} %get-tuple-element.666, s32[]{:T(128)} %get-tuple-element.665, bf16[12288,384]{1,0:T(8,128)(2,1)} %get-tuple-element.695, f32[256]{0:T(256)S(1)} %bitcast.268, s32[256]{0:T(256)S(1)} %bitcast.284, f32[256]{0:T(256)S(1)} %bitcast.254, s32[256]{0:T(256)S(1)} %bitcast.270, ...), kind=kOutput, calls=%fused_computation.56.clone.1 | convolution fusion | flops 2566914048 | bytes 9863680 | tf_op jit(solution)/shard_map/while/body/eval_jaxpr/dot_general | solution.py:67
  267.0 1.4 constant_dynamic-slice_fusion.7
  268.4 31.4 %fusion.159 = f32[6,256,384]{2,1,0:T(8,128)} fusion(f32[6,256,384]{2,1,0:T(8,128)} %get-tuple-element.666, s32[]{:T(128)} %get-tuple-element.665, bf16[12288,384]{1,0:T(8,128)(2,1)} %get-tuple-element.695, f32[256]{0:T(256)S(1)} %bitcast.268, s32[256]{0:T(256)S(1)} %bitcast.284, f32[256]{0:T(256)S(1)} %bitcast.254, s32[256]{0:T(256)S(1)} %bitcast.270, ...), kind=kOutput, calls=%fused_computation.56.clone.1 | convolution fusion | flops 2566914048 | bytes 9863680 | tf_op jit(solution)/shard_map/while/body/eval_jaxpr/dot_general | solution.py:67
  301.3 1.2 constant_dynamic-slice_fusion.7
  302.5 31.5 %fusion.159 = f32[6,256,384]{2,1,0:T(8,128)} fusion(f32[6,256,384]{2,1,0:T(8,128)} %get-tuple-element.666, s32[]{:T(128)} %get-tuple-element.665, bf16[12288,384]{1,0:T(8,128)(2,1)} %get-tuple-element.695, f32[256]{0:T(256)S(1)} %bitcast.268, s32[256]{0:T(256)S(1)} %bitcast.284, f32[256]{0:T(256)S(1)} %bitcast.254, s32[256]{0:T(256)S(1)} %bitcast.270, ...), kind=kOutput, calls=%fused_computation.56.clone.1 | convolution fusion | flops 2566914048 | bytes 9863680 | tf_op jit(solution)/shard_map/while/body/eval_jaxpr/dot_general | solution.py:67
  335.4 1.2 constant_dynamic-slice_fusion.7
  336.6 31.4 %fusion.159 = f32[6,256,384]{2,1,0:T(8,128)} fusion(f32[6,256,384]{2,1,0:T(8,128)} %get-tuple-element.666, s32[]{:T(128)} %get-tuple-element.665, bf16[12288,384]{1,0:T(8,128)(2,1)} %get-tuple-element.695, f32[256]{0:T(256)S(1)} %bitcast.268, s32[256]{0:T(256)S(1)} %bitcast.284, f32[256]{0:T(256)S(1)} %bitcast.254, s32[256]{0:T(256)S(1)} %bitcast.270, ...), kind=kOutput, calls=%fused_computation.56.clone.1 | convolution fusion | flops 2566914048 | bytes 9863680 | tf_op jit(solution)/shard_map/while/body/eval_jaxpr/dot_general | solution.py:67
  376.5 66.2 %while.25 = (s32[]{:T(128)}, f32[3,1536,128]{1,2,0:T(8,128)}, s32[3]{0:T(128)S(1)}, s32[16,384]{1,0:T(8,128)}, f32[16,384]{1,0:T(8,128)}, /*index=5*/bf16[1536,6...) while((s32[]{:T(128)}, f32[3,1536,128]{1,2,0:T(8,128)}, ...), condition=%wide.region_7.8_spmd.clone.clone, body=%wide.region_6.7_spmd.clone.clone.sunk | while | flops 2453667840 | bytes 19711052 | solution.py:82
  378.9 1.1 fusion.162
  380.0 18.5 %fusion.163 = f32[3,1536,128]{1,2,0:T(8,128)} fusion(f32[3,1536,128]{1,2,0:T(8,128)} %get-tuple-element.591, s32[]{:T(128)} %get-tuple-element.590, bf16[1536,6144]{1,0:T(8,128)(2,1)} %get-tuple-element.620, f32[128]{0:T(128)S(1)} %get-tuple-element.533, s32[128]{0:T(128)S(1)} %get-tuple-element.534, f32[128]{0:T(128)S(1)} %get-tuple-element.535, ...), kind=kOutput, calls=%fused_computation.78.clone.1 | convolution fusion | flops 2453667840 | bytes 19677696 | tf_op jit(solution)/shard_map/while/body/eval_jaxpr/dot_general | solution.py:78
  402.1 18.5 %fusion.163 = f32[3,1536,128]{1,2,0:T(8,128)} fusion(f32[3,1536,128]{1,2,0:T(8,128)} %get-tuple-element.591, s32[]{:T(128)} %get-tuple-element.590, bf16[1536,6144]{1,0:T(8,128)(2,1)} %get-tuple-element.620, f32[128]{0:T(128)S(1)} %get-tuple-element.533, s32[128]{0:T(128)S(1)} %get-tuple-element.534, f32[128]{0:T(128)S(1)} %get-tuple-element.535, ...), kind=kOutput, calls=%fused_computation.78.clone.1 | convolution fusion | flops 2453667840 | bytes 19677696 | tf_op jit(solution)/shard_map/while/body/eval_jaxpr/dot_general | solution.py:78
  424.1 18.5 %fusion.163 = f32[3,1536,128]{1,2,0:T(8,128)} fusion(f32[3,1536,128]{1,2,0:T(8,128)} %get-tuple-element.591, s32[]{:T(128)} %get-tuple-element.590, bf16[1536,6144]{1,0:T(8,128)(2,1)} %get-tuple-element.620, f32[128]{0:T(128)S(1)} %get-tuple-element.533, s32[128]{0:T(128)S(1)} %get-tuple-element.534, f32[128]{0:T(128)S(1)} %get-tuple-element.535, ...), kind=kOutput, calls=%fused_computation.78.clone.1 | convolution fusion | flops 2453667840 | bytes 19677696 | tf_op jit(solution)/shard_map/while/body/eval_jaxpr/dot_general | solution.py:78
  442.7 2.1 copy.28
  444.8 3.8 fusion.79
  448.6 2.5 reshape.133
  451.1 31.9 %all_to_all.11 = bf16[128,18,256]{2,1,0:T(8,128)(2,1)S(1)} all-to-all(bf16[128,18,256]{2,1,0:T(8,128)(2,1)S(1)} %reshape.133), channel_id=1, replica_groups=mesh['alpha'=8,'beta'=16] {'alpha','beta'}, dimensions={0} | all-to-all | bytes 2359296 | tf_op jit(solution)/shard_map/all_to_all | solution.py:135
  483.4 4.2 gather_fusion
  491.2 63.8 %all-reduce = (f32[]{:T(128)}, f32[]{:T(128)}) all-reduce(f32[]{:T(128)} %get-tuple-element.261, f32[]{:T(128)} %get-tuple-element.260), channel_id=1, replica_groups=mesh['alpha'=8,'beta'=16] {'alpha','beta'}, use_global_device_ids=true, to_apply=%region_9.10 | all-reduce | flops 2 | bytes 16 | tf_op jit(solution)/shard_map/psum | solution.py:147
  556.4 1.3 multiply_reduce_fusion
  557.7 62.8 %psum.23 = f32[]{:T(128)} all-reduce(f32[]{:T(128)} %get-tuple-element.290), channel_id=1, replica_groups=mesh['alpha'=8,'beta'=16] {'alpha','beta'}, use_global_device_ids=true, to_apply=%region_13.14 | all-reduce | flops 1 | bytes 8 | tf_op jit(solution)/shard_map/psum | solution.py:150
  (98 shorter events, 24.9 us)
Async XLA Ops:
  7.2 3.7 copy-start.2
  7.2 5.3 copy-start.4
  7.2 135.9 %all-gather.3.cloned.1.call-start = ((), (), s32[]{:S(2)}) async-start(), calls=%async_computation.2 | async-start | bytes 10616832 | tf_op jit(solution)/shard_map/all_gather | solution.py:122
  8.0 6.2 copy-start.14
  8.0 6.2 copy-start.16
  8.0 6.2 copy-start.18
  8.0 6.2 copy-start.12
  8.0 7.0 %copy-start.10 = (pred[768]{0:T(1024)(128)(4,1)}, pred[768]{0:T(1024)(128)(4,1)S(1)}, u32[]{:S(2)}) copy-start(pred[768]{0:T(1024)(128)(4,1)S(1)} %get-tuple-element.361) | copy-start | bytes 2308
  8.0 7.8 %copy-start.8 = (pred[768]{0:T(1024)(128)(4,1)}, pred[768]{0:T(1024)(128)(4,1)S(1)}, u32[]{:S(2)}) copy-start(pred[768]{0:T(1024)(128)(4,1)S(1)} %get-tuple-element.356) | copy-start | bytes 2308
  90.4 2.5 copy-start.7
  90.4 2.5 copy-start.21
  90.4 3.1 copy-start.6
  90.4 3.1 copy-start.20
  92.1 284.3 %all-gather.5.cloned.1.call-start = ((), (), s32[]{:S(2)}) async-start(), calls=%async_computation.3 | async-start | bytes 20054016 | tf_op jit(solution)/shard_map/all_gather | solution.py:130
  442.7 2.1 copy-start.1
  451.1 32.2 %copy-start = (s32[768]{0:T(1024)S(1)}, s32[768]{0:T(1024)}, u32[]{:S(2)}) copy-start(s32[768]{0:T(1024)} %get-tuple-element.262) | copy-start | bytes 9220
  483.1 4.5 copy-start.5
  483.1 4.6 copy-start.19
  483.1 5.1 copy-start.17
  483.3 5.3 copy-start.15
  483.3 5.8 copy-start.13
  483.4 6.3 copy-start.11
  483.4 6.8 %copy-start.3 = (f32[42,768]{1,0:T(8,128)S(1)}, f32[42,768]{1,0:T(8,128)}, u32[]{:S(2)}) copy-start(f32[42,768]{1,0:T(8,128)} %param.15) | copy-start | bytes 387076
  483.4 6.8 %copy-start.9 = (pred[768]{0:T(1024)(128)(4,1)S(1)}, pred[768]{0:T(1024)(128)(4,1)}, u32[]{:S(2)}) copy-start(pred[768]{0:T(1024)(128)(4,1)} %copy-done.8) | copy-start | bytes 2308
Sparse Core Ops, SparseCore 0:
  92.2 50.7 all-gather.2
  145.2 129.1 all-gather.4
where the time goes:
time: 637 us; the launch traced here: 629 us
  matrix products  254 us (40%)
  blocking collectives  194 us (30%)
  local copies, waits for them, and re-layouts  70.9 us (11%)
  waiting for transfers between devices  50.3 us (8%)
  loops' own time  33.5 us (5%)
  between operations  17.9 us (3%)
  other arithmetic  9.02 us (1%)
    dot_general x6, matrix products, alpha_one_block(): return jnp.dot(coupling, gathered, preferred_element_type=jnp.float32)  189 us
    psum x1, blocking collectives, body(): square_sum, cross_sum = lax.psum((own_square, own_cross), ('alpha', 'beta'))  63.8 us
    psum x1, blocking collectives, body(): residual_square = lax.psum(jnp.sum(residual * residual), ('alpha', 'beta'))  62.8 us
    dot_general x3, matrix products, beta_one_block(): lax.dot_general(gathered, coupling, (((1,), (1,)), ((), ())), preferred_e...  55.6 us
    all_gather x1, waiting for transfers between devices, body(): lax.all_gather(amplitude, 'alpha', axis=0, tiled=True)  49.5 us
    scatter x2, local copies, waits for them, and re-layouts, body(): outgoing = jnp.zeros((devices, capacity, det_width), jnp.bfloat16).at[tar...  38.3 us
    all_to_all x1, blocking collectives, body(): lax.all_to_all(outgoing, ('alpha', 'beta'), split_axis=0, concat_axis=0,...  35.2 us
    all_to_all x1, blocking collectives, body(): lax.all_to_all(sigma_grid.reshape(devices, capacity, det_width), ('alpha'...  31.9 us
  transfers between devices with their start and end apart: 2, of which 1 were waited for; matrix products, arithmetic and copies ran while one was open for 32% of the time, Pallas kernels for 0%

commit v1 on v0

--- a/solution.py
+++ b/solution.py
@@ -3,6 +3,13 @@
 import jax.numpy as jnp
 from jax import lax
 from jax.sharding import PartitionSpec as P
+
+
+def all_by_exchange(x, mesh_axis, along):
+    count = lax.axis_size(mesh_axis)
+    shards = jnp.stack([x for _ in range(count)])
+    shards = lax.all_to_all(shards, mesh_axis, split_axis=0, concat_axis=0)
+    return jnp.concatenate(shards, axis=along)
 
 
 def class_forward(coefs, classes, transforms):
@@ -119,7 +126,7 @@
         alpha_weights,
         math.gcd(rows_alpha, 256),
         jnp.zeros((rows_alpha, cols_beta), jnp.float32),
-        lax.all_gather(amplitude, "alpha", axis=0, tiled=True),
+        all_by_exchange(amplitude, "alpha", 0),
     )
     beta_weights = live_weights(beta_values, beta_counts)
     beta_term = beta_fold(

time: 637 us -> 697 us (1.094)
  waiting for transfers between devices: 50.3 us -> 104 us
    all_to_all x0 -> x1, waiting for transfers between devices: none -> 104 us  [all_by_exchange(): shards = lax.all_to_all(shards, mesh_axis, split_axis=0, concat_axis=0)]
    all_gather x1 -> x0, waiting for transfers between devices: 49.5 us -> none  [body(): lax.all_gather(amplitude, 'alpha', axis=0, tiled=True)]
  transfers between devices with their start and end apart: 2 -> 2, of which waited for: 1 -> 1; matrix products, arithmetic and copies ran while one was open for 32% -> 29% of each run, Pallas kernels for 0% -> 0%
where the time goes in v1:
time: 697 us; the launch traced here: 688 us
  matrix products  254 us (36%)
  blocking collectives  190 us (27%)
  waiting for transfers between devices  104 us (15%)
  local copies, waits for them, and re-layouts  73.9 us (11%)
  loops' own time  33.1 us (5%)
  between operations  17.9 us (3%)
  other arithmetic  9 us (1%)
    dot_general x6, matrix products, alpha_one_block(): return jnp.dot(coupling, gathered, preferred_element_type=jnp.float32)  189 us
    all_to_all x1, waiting for transfers between devices, all_by_exchange(): shards = lax.all_to_all(shards, mesh_axis, split_axis=0, concat_axis=0)  104 us
    psum x1, blocking collectives, body(): square_sum, cross_sum = lax.psum((own_square, own_cross), ('alpha', 'beta'))  63.8 us
    psum x1, blocking collectives, body(): residual_square = lax.psum(jnp.sum(residual * residual), ('alpha', 'beta'))  62.8 us
    dot_general x3, matrix products, beta_one_block(): lax.dot_general(gathered, coupling, (((1,), (1,)), ((), ())), preferred_e...  55.6 us
    scatter x2, local copies, waits for them, and re-layouts, body(): outgoing = jnp.zeros((devices, capacity, det_width), jnp.bfloat16).at[tar...  38.3 us
    all_to_all x1, blocking collectives, body(): lax.all_to_all(outgoing, ('alpha', 'beta'), split_axis=0, concat_axis=0,...  35.2 us
    another operation x1, loops' own time, alpha_fold(): lax.map(alpha_one_block, jnp.arange(summed.shape[0] // block_rows, dtype=...  31.2 us
  transfers between devices with their start and end apart: 2, of which 1 were waited for; matrix products, arithmetic and copies ran while one was open for 29% of the time, Pallas kernels for 0%

profile of v1, /device:TPU:1, one launch (start us, length us, event | category | flops | bytes accessed | tf_op | source)
XLA Modules:
  0.0 688.5 jit_solution(11514088856719967041)
XLA Ops:
  8.7 1.3 fusion.143
  10.8 1.6 fusion.97
  16.8 37.6 %scatter_fusion = bf16[128,18,256]{2,0,1:T(8,128)(2,1)S(1)} fusion(bf16[128,18,256]{2,0,1:T(8,128)(2,1)S(1)} %broadcast_in_dim.410, s32[768]{0:T(1024)S(1)} %get-tuple-element.263, bf16[768,256]{1,0:T(8,128)(2,1)S(1)} %fusion.80), kind=kCustom, calls=%fused_computation.1 | custom fusion | bytes 1185792 | tf_op jit(solution)/shard_map/scatter | solution.py:119
  55.1 35.2 %all_to_all.15 = bf16[128,18,256]{2,1,0:T(8,128)(2,1)S(1)} all-to-all(bf16[128,18,256]{2,1,0:T(8,128)(2,1)S(1)} %copy.27), channel_id=1, replica_groups=mesh['alpha'=8,'beta'=16] {'alpha','beta'}, dimensions={0} | all-to-all | bytes 2359296 | tf_op jit(solution)/shard_map/all_to_all | solution.py:121
  91.2 4.5 stack.3
  95.7 6.7 all-to-all-start.1
  103.7 103.6 %all-to-all-done.1 = bf16[8,1536,384]{2,1,0:T(8,128)(2,1)} async-done(((bf16[8,1536,384]{2,1,0:T(8,128)(2,1)}), bf16[8,1536,384]{2,1,0:T(8,128)(2,1)}, u32[]{:S(2)}, u32[]{:S(2)}) %all-to-all-start.1) | async-done | bytes 9437216 | tf_op jit(solution)/shard_map/all_to_all | solution.py:11
  207.3 232.0 %while.24 = (s32[]{:T(128)}, f32[6,256,384]{2,1,0:T(8,128)}, s32[6]{0:T(128)S(1)}, s32[16,1536]{1,0:T(8,128)}, f32[16,1536]{1,0:T(8,128)S(1)}, /*index=5*/bf16[1...) while((s32[]{:T(128)}, f32[6,256,384]{2,1,0:T(8,128)}, ...), condition=%wide.region_5.6_spmd.clone.clone, body=%wide.region_4.5_spmd.clone.clone.sunk | while | flops 2566914048 | bytes 9929303 | solution.py:76
  227.7 1.3 constant_dynamic-slice_fusion.7
  229.0 31.5 %fusion.159 = f32[6,256,384]{2,1,0:T(8,128)} fusion(f32[6,256,384]{2,1,0:T(8,128)} %get-tuple-element.666, s32[]{:T(128)S(6)} %copy.41, bf16[12288,384]{1,0:T(8,128)(2,1)} %get-tuple-element.695, f32[256]{0:T(256)S(1)} %bitcast.269, s32[256]{0:T(256)S(1)} %bitcast.285, f32[256]{0:T(256)S(1)} %bitcast.255, s32[256]{0:T(256)S(1)} %bitcast.271, ...), kind=kOutput, calls=%fused_computation.56.clone.1 | convolution fusion | flops 2566914048 | bytes 9863172 | tf_op jit(solution)/shard_map/while/body/eval_jaxpr/dot_general | solution.py:74
  261.9 1.4 constant_dynamic-slice_fusion.7
  263.3 31.4 %fusion.159 = f32[6,256,384]{2,1,0:T(8,128)} fusion(f32[6,256,384]{2,1,0:T(8,128)} %get-tuple-element.666, s32[]{:T(128)S(6)} %copy.41, bf16[12288,384]{1,0:T(8,128)(2,1)} %get-tuple-element.695, f32[256]{0:T(256)S(1)} %bitcast.269, s32[256]{0:T(256)S(1)} %bitcast.285, f32[256]{0:T(256)S(1)} %bitcast.255, s32[256]{0:T(256)S(1)} %bitcast.271, ...), kind=kOutput, calls=%fused_computation.56.clone.1 | convolution fusion | flops 2566914048 | bytes 9863172 | tf_op jit(solution)/shard_map/while/body/eval_jaxpr/dot_general | solution.py:74
  296.1 1.2 constant_dynamic-slice_fusion.7
  297.3 31.5 %fusion.159 = f32[6,256,384]{2,1,0:T(8,128)} fusion(f32[6,256,384]{2,1,0:T(8,128)} %get-tuple-element.666, s32[]{:T(128)S(6)} %copy.41, bf16[12288,384]{1,0:T(8,128)(2,1)} %get-tuple-element.695, f32[256]{0:T(256)S(1)} %bitcast.269, s32[256]{0:T(256)S(1)} %bitcast.285, f32[256]{0:T(256)S(1)} %bitcast.255, s32[256]{0:T(256)S(1)} %bitcast.271, ...), kind=kOutput, calls=%fused_computation.56.clone.1 | convolution fusion | flops 2566914048 | bytes 9863172 | tf_op jit(solution)/shard_map/while/body/eval_jaxpr/dot_general | solution.py:74
  330.1 1.2 constant_dynamic-slice_fusion.7
  331.3 31.4 %fusion.159 = f32[6,256,384]{2,1,0:T(8,128)} fusion(f32[6,256,384]{2,1,0:T(8,128)} %get-tuple-element.666, s32[]{:T(128)S(6)} %copy.41, bf16[12288,384]{1,0:T(8,128)(2,1)} %get-tuple-element.695, f32[256]{0:T(256)S(1)} %bitcast.269, s32[256]{0:T(256)S(1)} %bitcast.285, f32[256]{0:T(256)S(1)} %bitcast.255, s32[256]{0:T(256)S(1)} %bitcast.271, ...), kind=kOutput, calls=%fused_computation.56.clone.1 | convolution fusion | flops 2566914048 | bytes 9863172 | tf_op jit(solution)/shard_map/while/body/eval_jaxpr/dot_general | solution.py:74
  364.1 1.4 constant_dynamic-slice_fusion.7
  365.5 31.5 %fusion.159 = f32[6,256,384]{2,1,0:T(8,128)} fusion(f32[6,256,384]{2,1,0:T(8,128)} %get-tuple-element.666, s32[]{:T(128)S(6)} %copy.41, bf16[12288,384]{1,0:T(8,128)(2,1)} %get-tuple-element.695, f32[256]{0:T(256)S(1)} %bitcast.269, s32[256]{0:T(256)S(1)} %bitcast.285, f32[256]{0:T(256)S(1)} %bitcast.255, s32[256]{0:T(256)S(1)} %bitcast.271, ...), kind=kOutput, calls=%fused_computation.56.clone.1 | convolution fusion | flops 2566914048 | bytes 9863172 | tf_op jit(solution)/shard_map/while/body/eval_jaxpr/dot_general | solution.py:74
  398.3 1.2 constant_dynamic-slice_fusion.7
  399.5 31.5 %fusion.159 = f32[6,256,384]{2,1,0:T(8,128)} fusion(f32[6,256,384]{2,1,0:T(8,128)} %get-tuple-element.666, s32[]{:T(128)S(6)} %copy.41, bf16[12288,384]{1,0:T(8,128)(2,1)} %get-tuple-element.695, f32[256]{0:T(256)S(1)} %bitcast.269, s32[256]{0:T(256)S(1)} %bitcast.285, f32[256]{0:T(256)S(1)} %bitcast.255, s32[256]{0:T(256)S(1)} %bitcast.271, ...), kind=kOutput, calls=%fused_computation.56.clone.1 | convolution fusion | flops 2566914048 | bytes 9863172 | tf_op jit(solution)/shard_map/while/body/eval_jaxpr/dot_general | solution.py:74
  439.4 66.2 %while.25 = (s32[]{:T(128)}, f32[3,1536,128]{1,2,0:T(8,128)}, s32[3]{0:T(128)S(1)}, s32[16,384]{1,0:T(8,128)}, f32[16,384]{1,0:T(8,128)}, /*index=5*/bf16[1536,6...) while((s32[]{:T(128)}, f32[3,1536,128]{1,2,0:T(8,128)}, ...), condition=%wide.region_7.8_spmd.clone.clone, body=%wide.region_6.7_spmd.clone.clone.sunk | while | flops 2453667840 | bytes 19710552 | solution.py:89
  442.9 18.5 %fusion.163 = f32[3,1536,128]{1,2,0:T(8,128)} fusion(f32[3,1536,128]{1,2,0:T(8,128)} %get-tuple-element.591, s32[]{:T(128)S(6)} %copy.35, bf16[1536,6144]{1,0:T(8,128)(2,1)} %get-tuple-element.620, f32[128]{0:T(128)S(1)} %get-tuple-element.533, s32[128]{0:T(128)S(1)} %get-tuple-element.534, f32[128]{0:T(128)S(1)} %get-tuple-element.535, ...), kind=kOutput, calls=%fused_computation.78.clone.1 | convolution fusion | flops 2453667840 | bytes 19677188 | tf_op jit(solution)/shard_map/while/body/eval_jaxpr/dot_general | solution.py:85
  465.0 18.5 %fusion.163 = f32[3,1536,128]{1,2,0:T(8,128)} fusion(f32[3,1536,128]{1,2,0:T(8,128)} %get-tuple-element.591, s32[]{:T(128)S(6)} %copy.35, bf16[1536,6144]{1,0:T(8,128)(2,1)} %get-tuple-element.620, f32[128]{0:T(128)S(1)} %get-tuple-element.533, s32[128]{0:T(128)S(1)} %get-tuple-element.534, f32[128]{0:T(128)S(1)} %get-tuple-element.535, ...), kind=kOutput, calls=%fused_computation.78.clone.1 | convolution fusion | flops 2453667840 | bytes 19677188 | tf_op jit(solution)/shard_map/while/body/eval_jaxpr/dot_general | solution.py:85
  487.0 18.5 %fusion.163 = f32[3,1536,128]{1,2,0:T(8,128)} fusion(f32[3,1536,128]{1,2,0:T(8,128)} %get-tuple-element.591, s32[]{:T(128)S(6)} %copy.35, bf16[1536,6144]{1,0:T(8,128)(2,1)} %get-tuple-element.620, f32[128]{0:T(128)S(1)} %get-tuple-element.533, s32[128]{0:T(128)S(1)} %get-tuple-element.534, f32[128]{0:T(128)S(1)} %get-tuple-element.535, ...), kind=kOutput, calls=%fused_computation.78.clone.1 | convolution fusion | flops 2453667840 | bytes 19677188 | tf_op jit(solution)/shard_map/while/body/eval_jaxpr/dot_general | solution.py:85
  505.6 2.1 copy.28
  507.7 3.8 fusion.79
  511.5 2.5 reshape.136
  514.0 28.1 %all_to_all.16 = bf16[128,18,256]{2,1,0:T(8,128)(2,1)S(1)} all-to-all(bf16[128,18,256]{2,1,0:T(8,128)(2,1)S(1)} %reshape.136), channel_id=1, replica_groups=mesh['alpha'=8,'beta'=16] {'alpha','beta'}, dimensions={0} | all-to-all | bytes 2359296 | tf_op jit(solution)/shard_map/all_to_all | solution.py:142
  542.4 4.2 gather_fusion
  550.3 63.8 %all-reduce = (f32[]{:T(128)}, f32[]{:T(128)}) all-reduce(f32[]{:T(128)} %get-tuple-element.261, f32[]{:T(128)} %get-tuple-element.260), channel_id=1, replica_groups=mesh['alpha'=8,'beta'=16] {'alpha','beta'}, use_global_device_ids=true, to_apply=%region_9.10 | all-reduce | flops 2 | bytes 16 | tf_op jit(solution)/shard_map/psum | solution.py:154
  615.4 1.3 multiply_reduce_fusion
  616.7 62.8 %psum.23 = f32[]{:T(128)} all-reduce(f32[]{:T(128)} %get-tuple-element.290), channel_id=1, replica_groups=mesh['alpha'=8,'beta'=16] {'alpha','beta'}, use_global_device_ids=true, to_apply=%region_13.14 | all-reduce | flops 1 | bytes 8 | tf_op jit(solution)/shard_map/psum | solution.py:157
  (100 shorter events, 26.5 us)
Async XLA Ops:
  7.2 3.6 copy-start.3
  7.2 5.2 copy-start.5
  10.7 4.2 copy-start.13
  10.7 4.2 copy-start.15
  10.7 4.2 copy-start.17
  10.7 4.2 copy-start.19
  10.7 4.2 copy-start.11
  10.8 5.0 copy-start.9
  91.2 4.5 copy-start.1
  95.7 7.4 %copy-start.8 = (bf16[16,384]{1,0:T(8,128)(2,1)S(1)}, bf16[16,384]{1,0:T(8,128)(2,1)}, u32[]{:S(2)}) copy-start(bf16[16,384]{1,0:T(8,128)(2,1)} %param.23) | copy-start | bytes 36868
  95.7 7.4 %copy-start.22 = (s32[384]{0:T(512)S(1)}, s32[384]{0:T(512)}, u32[]{:S(2)}) copy-start(s32[384]{0:T(512)} %param.24) | copy-start | bytes 4612
  95.7 8.0 %copy-start.7 = (bf16[16,1536]{1,0:T(8,128)(2,1)S(1)}, bf16[16,1536]{1,0:T(8,128)(2,1)}, u32[]{:S(2)}) copy-start(bf16[16,1536]{1,0:T(8,128)(2,1)} %param.20) | copy-start | bytes 147460
  95.7 8.0 %copy-start.21 = (s32[1536]{0:T(1024)S(1)}, s32[1536]{0:T(1024)}, u32[]{:S(2)}) copy-start(s32[1536]{0:T(1024)} %param.21) | copy-start | bytes 18436
  95.7 111.6 %all-to-all-start.1 = ((bf16[8,1536,384]{2,1,0:T(8,128)(2,1)}), bf16[8,1536,384]{2,1,0:T(8,128)(2,1)}, u32[]{:S(2)}, u32[]{:S(2)}) async-start(bf16[8,1536,384]{2,1,0:T(8,128)(2,1)} %stack.3), calls=%async_computation.1 | async-start | bytes 18874368 | tf_op jit(solution)/shard_map/all_to_all | solution.py:11
  102.4 337.0 %all-gather.2.cloned.1.call-start = ((), (), s32[]{:S(2)}) async-start(), calls=%async_computation.3 | async-start | bytes 20054016 | tf_op jit(solution)/shard_map/all_gather | solution.py:137
  505.6 2.1 copy-start.2
  514.0 28.4 %copy-start = (s32[768]{0:T(1024)S(1)}, s32[768]{0:T(1024)}, u32[]{:S(2)}) copy-start(s32[768]{0:T(1024)} %get-tuple-element.262) | copy-start | bytes 9220
  542.1 4.5 copy-start.6
  542.1 4.6 copy-start.20
  542.1 5.1 copy-start.18
  542.4 5.3 copy-start.16
  542.4 5.8 copy-start.14
  542.4 6.3 copy-start.12
  542.4 6.8 copy-start.4
  542.4 6.8 copy-start.10
Sparse Core Ops, SparseCore 0:
  105.3 126.2 all-gather.1
